TPU v7x, 512 devices: a whole 4x8x8 slice. The times are simulated.
512 devices in a mesh: dp: 128 (over y, z, core), mp: 4 (over x).
Axes of the slice: x: 4, y: 8, z: 8, core: 2. Of those that a mesh axis runs over, the one named last changes fastest.
Arguments:
- frames: bfloat16 [32768, 1024], P('dp'), may hold values from -24 to 24
- proj_in: bfloat16 [1024, 2, 1024], P(None, None, 'mp'), may hold values from -0.1875 to 0.1875
- depthwise: float32 [31, 1024], P(None, 'mp'), may hold values from -1 to 1
- bn_gain: float32 [1024], P('mp'), may hold values from 0.5 to 1.5
- bn_shift: float32 [1024], P('mp'), may hold values from -3 to 3
- proj_out: bfloat16 [1024, 1024], P(None, 'mp'), may hold values from -0.1875 to 0.1875
- grad_out: bfloat16 [32768, 1024], P('dp'), may hold values from -24 to 24
- counts: int32 [128], replicated, may hold values from 1 to 2, as said below
- lengths: int32 [128, 2], P('dp'), may hold values from 1 to 255, as said below
Outputs:
- frame_grad: bfloat16 [32768, 1024], P('dp', 'mp')
- in_grad: float32 [1024, 2, 1024], P('dp', None, 'mp')
- out_grad: float32 [1024, 1024], P('dp', 'mp')
- depth_grad: float32 [31, 1024], P(None, 'mp')
- gain_grad: float32 [1024], P('mp')
- shift_grad: float32 [1024], P('mp')
Inputs may be any that keep to these rules, and one draw needn't show every extreme that they name: `counts`: some device holds 2 live blocks. lengths[d] sums to 128 * counts[d]; on some device with 2 live blocks one utterance holds all frames but one for each other utterance.
All inputs are finite; a program needn't handle non-finite values.
Results may differ from a plain program's by a relative error of at most 0.0095.
Values may be sent and summed in bfloat16 or wider, within the bound.
No kernel may reach another device: no remote copies, remote signals or barrier semaphores. Data moves between devices by JAX's collectives and lax.ppermute only.
A program may use at most 64 MiB of HBM per device.

v0:
```python
import jax
import jax.numpy as jnp
from jax import lax
from jax.sharding import PartitionSpec as P

BLOCK = 128


def time_shift(values, offset, fill_value):
    if offset > 0:
        pad_part = jnp.full((offset,) + values.shape[1:], fill_value, values.dtype)
        return jnp.concatenate([values[offset:], pad_part], axis=0)
    if offset < 0:
        pad_part = jnp.full((-offset,) + values.shape[1:], fill_value, values.dtype)
        return jnp.concatenate([pad_part, values[:offset]], axis=0)
    return values


def tap_term(glu_float, owner_id, live_col, offset):
    same_utt = (time_shift(owner_id, offset, -1) == owner_id).astype(jnp.float32)[
        :, None
    ] * live_col
    return time_shift(glu_float, offset, 0.0) * same_utt


def shards(frames, proj_in, depthwise, bn_gain, bn_shift, proj_out, grad_out, counts, lengths):
    frames_dev = frames.shape[0]
    model_width = frames.shape[1]
    channels = proj_in.shape[2]
    tap_count = depthwise.shape[0]
    radius = tap_count // 2
    rows_dev = model_width // lax.axis_size("dp")
    position = jnp.arange(frames_dev, dtype=jnp.int32)
    utt_ends = jnp.cumsum(lengths[0])
    owner_id = jnp.sum((position[:, None] >= utt_ends[None, :]).astype(jnp.int32), axis=1)
    my_count = counts[lax.axis_index("dp")]
    live_col = (position < my_count * BLOCK).astype(jnp.float32)[:, None]
    frame_total = (jnp.sum(counts) * BLOCK).astype(jnp.float32)
    proj_flat = proj_in.reshape(model_width, 2 * channels)
    pre_act = jnp.dot(frames, proj_flat, preferred_element_type=jnp.float32)
    value_half = pre_act[:, :channels]
    gate_sig = jax.nn.sigmoid(pre_act[:, channels:])
    glu_out = (value_half * gate_sig * live_col).astype(jnp.bfloat16)
    glu_float = lax.optimization_barrier(glu_out).astype(jnp.float32)
    conv_out = jnp.zeros((frames_dev, channels), jnp.float32)
    for tap_index in range(tap_count):
        conv_out = conv_out + depthwise[tap_index] * tap_term(
            glu_float, owner_id, live_col, tap_index - radius
        )
    sum_val, sum_sq = lax.psum(
        (jnp.sum(conv_out, axis=0), jnp.sum(conv_out * conv_out, axis=0)), "dp"
    )
    mean_val = sum_val / frame_total
    square_mean = sum_sq / frame_total
    inv_std = lax.rsqrt(square_mean - mean_val * mean_val + 1e-05)
    normed = (conv_out - mean_val) * inv_std
    scaled = normed * bn_gain + bn_shift
    sig_scaled = jax.nn.sigmoid(scaled)
    hidden = (scaled * sig_scaled * live_col).astype(jnp.bfloat16)
    grad_hidden = jnp.dot(grad_out, proj_out, preferred_element_type=jnp.float32) * live_col
    grad_scaled = grad_hidden * sig_scaled * (1.0 + scaled * (1.0 - sig_scaled))
    local_shift = jnp.sum(grad_scaled, axis=0)
    local_gain = jnp.sum(grad_scaled * normed, axis=0)
    shift_grad, gain_grad = lax.psum((local_shift, local_gain), "dp")
    grad_conv = (
        live_col
        * bn_gain
        * inv_std
        * (grad_scaled - shift_grad / frame_total - normed * gain_grad / frame_total)
    )
    depth_rows = []
    for tap_index in range(tap_count):
        depth_rows.append(
            jnp.sum(grad_conv * tap_term(glu_float, owner_id, live_col, tap_index - radius), axis=0)
        )
    depth_grad = lax.psum(jnp.stack(depth_rows), "dp")
    grad_glu = jnp.zeros((frames_dev, channels), jnp.float32)
    for tap_index in range(tap_count):
        offset = tap_index - radius
        back_same = (time_shift(owner_id, -offset, -1) == owner_id).astype(jnp.float32)[
            :, None
        ] * live_col
        grad_glu = grad_glu + depthwise[tap_index] * time_shift(grad_conv, -offset, 0.0) * back_same
    grad_value = grad_glu * gate_sig
    grad_gate = grad_glu * value_half * gate_sig * (1.0 - gate_sig)
    grad_flat = jnp.concatenate([grad_value, grad_gate], axis=1).astype(jnp.bfloat16)
    frame_term = lax.dot_general(
        grad_flat, proj_flat, (((1,), (1,)), ((), ())), preferred_element_type=jnp.float32
    )
    frame_grad = lax.psum_scatter(
        frame_term.astype(jnp.bfloat16), "mp", scatter_dimension=1, tiled=True
    )
    summed = lax.psum_scatter(
        jnp.concatenate(
            [
                lax.dot_general(
                    frames, grad_flat, (((0,), (0,)), ((), ())), preferred_element_type=jnp.float32
                ),
                lax.dot_general(
                    grad_out, hidden, (((0,), (0,)), ((), ())), preferred_element_type=jnp.float32
                ),
            ],
            axis=1,
        ),
        "dp",
        scatter_dimension=0,
        tiled=True,
    )
    in_flat = summed[:, : 2 * channels]
    out_grad = summed[:, 2 * channels :]
    in_grad = in_flat.reshape(rows_dev, 2, channels)
    return (frame_grad, in_grad, out_grad, depth_grad, gain_grad, shift_grad)


def solution(mesh):
    placed = (
        P("dp", None),
        P(None, None, "mp"),
        P(None, "mp"),
        P("mp"),
        P("mp"),
        P(None, "mp"),
        P("dp", None),
        P(),
        P("dp", None),
    )
    return jax.shard_map(
        shards,
        mesh=mesh,
        in_specs=placed,
        out_specs=(
            P("dp", "mp"),
            P("dp", None, "mp"),
            P("dp", "mp"),
            P(None, "mp"),
            P("mp"),
            P("mp"),
        ),
        check_vma=False,
    )
```

profile of v0, /device:TPU:4, one launch (start us, length us, event | category | flops | bytes accessed | tf_op | source)
XLA Modules:
  0.0 1084.7 jit_solution(16203160187497668343)
XLA Ops:
  7.2 0.9 reduce-window.8
  8.2 0.7 fusion.86
  8.9 0.6 fusion.93
  9.5 0.6 fusion.85
  10.1 0.6 fusion.92
  10.8 0.6 fusion.84
  11.4 0.7 fusion.90
  12.1 0.7 fusion.83
  12.7 0.6 fusion.88
  13.4 0.6 fusion.82
  14.0 0.6 fusion.91
  14.7 0.6 fusion.81
  15.3 0.6 fusion.80
  15.9 0.6 fusion.79
  16.6 0.6 fusion.87
  17.2 0.6 fusion.89
  17.8 1.6 fusion.78
  19.4 1.7 fusion.77
  21.0 1.4 reduce_sum.335
  22.4 1.2 dynamic_slice.3
  24.2 1.4 copy.25
  25.7 0.4 fusion.94
  26.1 0.1 multiply_convert_fusion.3
  26.2 0.8 fusion.69
  27.1 0.9 fusion.68
  27.9 0.8 fusion.67
  28.7 0.8 fusion.66
  29.6 0.8 fusion.65
  30.4 0.8 fusion.64
  31.2 0.8 fusion.63
  32.0 0.9 fusion.62
  32.9 0.8 fusion.71
  33.7 0.7 fusion.70
  34.4 0.8 fusion.73
  35.2 0.7 fusion.72
  35.9 0.9 fusion.76
  36.8 0.8 fusion.75
  37.6 0.7 fusion.74
  39.0 0.9 fusion.14
  40.1 0.9 fusion.13
  41.1 6.2 multiply_reduce_fusion.32
  47.6 258.3 %all-reduce.89 = (f32[256]{0:T(256)S(1)}, f32[256]{0:T(256)S(1)}) all-reduce(f32[256]{0:T(256)} %get-tuple-element.58, f32[256]{0:T(256)S(1)} %get-tuple-element.57), channel_id=1, replica_groups=mesh['dp'=128,'mp'=4] {'dp'}, use_global_device_ids=true, to_apply=%region_6.7 | all-reduce | flops 512 | bytes 4096 | tf_op jit(solution)/shard_map/psum | solution.py:50
  306.0 2.3 fusion.46
  308.3 247.3 %all-reduce.88 = (f32[256]{0:T(256)}, f32[256]{0:T(256)S(1)}) all-reduce(f32[256]{0:T(256)S(1)} %get-tuple-element.56, f32[256]{0:T(256)S(1)} %get-tuple-element.55), channel_id=1, replica_groups=mesh['dp'=128,'mp'=4] {'dp'}, use_global_device_ids=true, to_apply=%region_10.11 | all-reduce | flops 512 | bytes 4096 | tf_op jit(solution)/shard_map/psum | solution.py:64
  555.6 0.6 copy-done.85
  556.2 2.9 multiply_reduce_fusion
  560.2 0.3 copy-done.13
  560.5 1.5 convolution_bitcast_fusion.1
  562.3 3.4 multiply_convert_fusion.2
  565.9 0.5 copy-done.12
  566.4 0.1 copy-done.11
  566.5 0.5 convolution_bitcast_fusion
  567.0 1.9 pad_maximum_fusion
  568.9 3.5 copy.21
  572.5 2.3 convolution_convert_fusion
  574.8 2.3 multiply_reduce_fusion.27
  577.2 2.5 multiply_reduce_fusion.18
  579.7 1.1 multiply_reduce_fusion.9
  580.9 2.8 stack.127
  583.7 491.3 %psum.39 = f32[31,256]{1,0:T(8,128)} all-reduce(f32[31,256]{1,0:T(8,128)S(1)} %stack.127), channel_id=1, replica_groups=mesh['dp'=128,'mp'=4] {'dp'}, use_global_device_ids=true, to_apply=%region_44.45 | all-reduce | flops 7936 | bytes 63488 | tf_op jit(solution)/shard_map/psum | solution.py:76
  1075.0 0.7 slice.683
  1075.7 0.1 copy.23
  1075.9 0.7 copy.19
  1076.6 1.3 slice.684
  (194 shorter events, 1.2 us)
Async XLA Ops:
  7.2 18.5 %copy-start = (bf16[256,1024]{1,0:T(8,128)(2,1)S(1)}, bf16[256,1024]{1,0:T(8,128)(2,1)}, u32[]{:S(2)}) copy-start(bf16[256,1024]{1,0:T(8,128)(2,1)} %param.9) | copy-start | bytes 1572868
  7.2 1067.8 %reduce-scatter.7.cloned.1.call-start = ((), (), s32[]{:S(2)}) async-start(), calls=%async_computation.3 | async-start | bytes 3170304
  38.4 9.0 copy-start.1
  39.9 7.4 copy-start.28
  39.9 7.4 copy-start.30
  40.0 7.4 copy-start.33
  40.0 7.4 copy-start.36
  40.0 7.4 copy-start.38
  40.0 7.4 copy-start.40
  40.0 7.4 copy-start.42
  40.0 7.4 copy-start.44
  40.0 7.4 copy-start.46
  40.0 7.4 copy-start.48
  40.0 7.4 copy-start.50
  40.0 7.4 copy-start.52
  40.1 7.4 copy-start.54
  40.1 7.4 copy-start.56
  41.0 6.5 copy-start.14
  41.0 6.5 copy-start.16
  41.0 6.5 copy-start.18
  41.0 6.5 copy-start.20
  41.0 6.5 copy-start.22
  41.0 6.5 copy-start.24
  41.0 6.5 copy-start.26
  41.0 6.5 copy-start.58
  41.0 6.5 copy-start.60
  41.1 6.5 copy-start.62
  41.1 6.5 copy-start.64
  41.1 6.5 copy-start.66
  41.1 6.5 copy-start.68
  41.1 6.5 copy-start.70
  305.9 249.7 %copy-start.84 = (f32[256]{0:T(256)}, f32[256]{0:T(256)S(1)}, u32[]{:S(2)}) copy-start(f32[256]{0:T(256)S(1)} %get-tuple-element.67) | copy-start | bytes 3076
  305.9 253.2 %copy-start.83 = (f32[256]{0:T(256)}, f32[256]{0:T(256)S(1)}, u32[]{:S(2)}) copy-start(f32[256]{0:T(256)S(1)} %get-tuple-element.66) | copy-start | bytes 3076
  559.6 2.3 copy-start.15
  559.6 2.3 copy-start.17
  559.6 2.3 copy-start.19
  559.6 2.3 copy-start.21
  559.7 2.3 copy-start.23
  559.7 2.3 copy-start.25
  559.7 2.3 copy-start.27
  559.7 2.3 copy-start.29
  559.7 2.3 copy-start.31
  559.7 2.3 copy-start.34
  559.7 2.3 copy-start.37
  559.7 2.3 copy-start.39
  559.7 2.3 copy-start.41
  559.7 2.3 copy-start.43
  559.8 2.3 copy-start.45
  559.8 2.3 copy-start.47
  559.8 2.3 copy-start.49
  559.8 2.3 copy-start.51
  559.8 2.3 copy-start.53
  572.4 4.8 copy-start.2
  572.4 4.8 copy-start.35
  572.4 7.3 copy-start.3
  572.4 7.3 copy-start.32
  572.4 505.5 %reduce-scatter.5.cloned.1.call-start = ((), (), s32[]{:S(2)}) async-start(), calls=%async_computation.2 | async-start | bytes 655360 | tf_op jit(solution)/shard_map/reduce_scatter | solution.py:90
  574.8 4.9 copy-start.4
  574.8 4.9 copy-start.5
  574.8 4.9 copy-start.6
  574.8 4.9 copy-start.7
  574.8 4.9 copy-start.8
  574.8 4.9 copy-start.9
  574.8 4.9 copy-start.10
  (24 other events, 49.6 us)
Sparse Core Ops, SparseCore 0:
  572.5 194.4 reduce-scatter.6
  770.4 22.4 reduce-scatter.4
where the time goes:
time: 1090 us; the launch traced here: 1080 us
  blocking collectives  997 us (91%)
  local copies, waits for them, and re-layouts  39.2 us (4%)
  other arithmetic  24.7 us (2%)
  between operations  16.7 us (2%)
    psum x1, blocking collectives, shards(): depth_grad = lax.psum(jnp.stack(depth_rows), 'dp')  491 us
    psum x1, blocking collectives, shards(): lax.psum((jnp.sum(conv_out, axis=0), jnp.sum(conv_out * conv_out, axis=0)...  258 us
    psum x1, blocking collectives, shards(): shift_grad, gain_grad = lax.psum((local_shift, local_gain), 'dp')  247 us
  transfers between devices with their start and end apart: 2, of which 0 were waited for; matrix products, arithmetic and copies ran while one was open for 1% of the time, Pallas kernels for 0%

commit v1 on v0

--- a/solution.py
+++ b/solution.py
@@ -73,7 +73,9 @@
         depth_rows.append(
             jnp.sum(grad_conv * tap_term(glu_float, owner_id, live_col, tap_index - radius), axis=0)
         )
-    depth_grad = lax.psum(jnp.stack(depth_rows), "dp")
+    x = jnp.stack(depth_rows)
+    parts = lax.all_gather(x, "dp", axis=0, tiled=False)
+    depth_grad = parts.sum(axis=0)
     grad_glu = jnp.zeros((frames_dev, channels), jnp.float32)
     for tap_index in range(tap_count):
         offset = tap_index - radius

time: 1090 us -> 887 us (0.81)
  the two profiles are of different devices: /device:TPU:4 before, /device:TPU:8 now
where the time goes in v1:
time: 887 us; the launch traced here: 886 us
  blocking collectives  470 us (53%)
  waiting for transfers between devices  323 us (36%)
  local copies, waits for them, and re-layouts  41.4 us (5%)
  other arithmetic  27.8 us (3%)
  between operations  16.5 us (2%)
    psum x1, blocking collectives, shards(): shift_grad, gain_grad = lax.psum((local_shift, local_gain), 'dp')  247 us
    psum x1, blocking collectives, shards(): lax.psum((jnp.sum(conv_out, axis=0), jnp.sum(conv_out * conv_out, axis=0)...  223 us
    unnamed x4, waiting for transfers between devices  216 us
    all_gather x1, waiting for transfers between devices, shards(): parts = lax.all_gather(x, 'dp', axis=0, tiled=False)  82.4 us
    reduce_scatter x1, waiting for transfers between devices, shards(): lax.psum_scatter(frame_term.astype(jnp.bfloat16), 'mp', scatter_dimension...  24.6 us
    slice x29, local copies, waits for them, and re-layouts, time_shift(): return jnp.concatenate([pad_part, values[:offset]], axis=0)  20.8 us
  transfers between devices with their start and end apart: 3, of which 3 were waited for; matrix products, arithmetic and copies ran while one was open for 2% of the time, Pallas kernels for 0%

profile of v1, /device:TPU:8, one launch (start us, length us, event | category | flops | bytes accessed | tf_op | source)
XLA Modules:
  0.0 885.7 jit_solution(5260216377612932720)
XLA Ops:
  7.2 0.9 reduce-window.8
  8.2 0.7 fusion.86
  8.9 0.6 fusion.93
  9.4 0.6 fusion.85
  10.0 0.6 fusion.92
  10.7 0.6 fusion.84
  11.3 0.7 fusion.90
  11.9 0.6 fusion.83
  12.6 0.6 fusion.88
  13.2 0.6 fusion.82
  13.8 0.6 fusion.91
  14.4 0.6 fusion.81
  15.0 0.6 fusion.80
  15.7 0.7 fusion.79
  16.3 0.6 fusion.87
  17.0 0.6 fusion.89
  17.6 1.6 fusion.78
  19.2 1.7 fusion.77
  20.9 1.4 reduce_sum.344
  22.3 1.2 dynamic_slice.3
  24.1 1.4 copy.25
  25.6 0.4 fusion.94
  26.2 0.8 fusion.69
  27.0 0.8 fusion.68
  27.8 0.8 fusion.67
  28.6 0.8 fusion.66
  29.5 0.8 fusion.65
  30.3 0.8 fusion.64
  31.1 0.8 fusion.63
  32.0 0.8 fusion.62
  32.8 0.7 fusion.71
  33.5 0.7 fusion.70
  34.3 0.7 fusion.73
  35.0 0.7 fusion.72
  35.7 0.9 fusion.76
  36.6 0.8 fusion.75
  37.4 0.7 fusion.74
  38.9 0.9 fusion.14
  39.9 0.9 fusion.13
  40.9 6.2 multiply_reduce_fusion.32
  47.4 222.9 %all-reduce.89 = (f32[256]{0:T(256)S(1)}, f32[256]{0:T(256)S(1)}) all-reduce(f32[256]{0:T(256)} %get-tuple-element.58, f32[256]{0:T(256)S(1)} %get-tuple-element.57), channel_id=1, replica_groups=mesh['dp'=128,'mp'=4] {'dp'}, use_global_device_ids=true, to_apply=%region_6.7 | all-reduce | flops 512 | bytes 4096 | tf_op jit(solution)/shard_map/psum | solution.py:50
  270.3 2.3 fusion.46
  272.6 247.4 %all-reduce.88 = (f32[256]{0:T(256)}, f32[256]{0:T(256)S(1)}) all-reduce(f32[256]{0:T(256)S(1)} %get-tuple-element.56, f32[256]{0:T(256)S(1)} %get-tuple-element.55), channel_id=1, replica_groups=mesh['dp'=128,'mp'=4] {'dp'}, use_global_device_ids=true, to_apply=%region_10.11 | all-reduce | flops 512 | bytes 4096 | tf_op jit(solution)/shard_map/psum | solution.py:64
  520.0 0.6 copy-done.85
  520.5 2.9 multiply_reduce_fusion
  524.6 0.3 copy-done.13
  524.8 1.5 convolution_bitcast_fusion.1
  526.7 3.4 multiply_convert_fusion.2
  530.2 0.5 copy-done.12
  530.9 0.5 convolution_bitcast_fusion
  531.3 1.9 pad_maximum_fusion
  533.2 3.6 copy.21
  536.9 2.3 multiply_reduce_fusion.27
  539.2 2.5 multiply_reduce_fusion.18
  541.8 1.1 multiply_reduce_fusion.9
  542.9 5.2 stack.127
  548.3 2.2 convolution_convert_fusion
  550.5 215.7 %reduce-scatter.7.cloned.1.call-done = f32[8,768]{1,0:T(8,128)} async-done(((f32[1024,768]{1,0:T(8,128)}), f32[8,768]{1,0:T(8,128)}) %reduce-scatter.7.cloned.1.call-update) | async-done | bytes 24592
  766.2 0.7 slice.683
  767.0 0.7 copy.19
  767.8 1.3 slice.684
  769.1 82.4 %all-gather.4.cloned.1.call-done = f32[128,31,256]{2,1,0:T(8,128)} async-done(((f32[1,31,256]{2,1,0:T(8,128)}), f32[128,31,256]{2,1,0:T(8,128)}) %all-gather.4.cloned.1.call-update) | async-done | bytes 4063248 | tf_op jit(solution)/shard_map/all_gather | solution.py:77
  851.5 3.1 reduce_sum.379
  854.6 24.6 %reduce-scatter.5.cloned.1.call-done = bf16[256,256]{1,0:T(8,128)(2,1)} async-done(((bf16[256,1024]{1,0:T(8,128)(2,1)}), bf16[256,256]{1,0:T(8,128)(2,1)}) %reduce-scatter.5.cloned.1.call-update) | async-done | bytes 131088 | tf_op jit(solution)/shard_map/reduce_scatter | solution.py:92
  (197 shorter events, 1.6 us)
Async XLA Ops:
  7.2 18.4 %copy-start = (bf16[256,1024]{1,0:T(8,128)(2,1)S(1)}, bf16[256,1024]{1,0:T(8,128)(2,1)}, u32[]{:S(2)}) copy-start(bf16[256,1024]{1,0:T(8,128)(2,1)} %param.9) | copy-start | bytes 1572868
  7.2 759.0 %reduce-scatter.7.cloned.1.call-start = ((), (), s32[]{:S(2)}) async-start(), calls=%async_computation.4 | async-start | bytes 3170304
  38.2 9.0 %copy-start.1 = (f32[253,256]{1,0:T(8,128)}, f32[253,256]{1,0:T(8,128)S(1)}, u32[]{:S(2)}) copy-start(f32[253,256]{1,0:T(8,128)S(1)} %get-tuple-element.123) | copy-start | bytes 777220
  39.7 7.4 copy-start.28
  39.8 7.4 copy-start.30
  39.8 7.4 copy-start.33
  39.8 7.4 copy-start.36
  39.8 7.4 copy-start.38
  39.8 7.4 copy-start.40
  39.8 7.4 copy-start.42
  39.8 7.4 copy-start.44
  39.8 7.4 copy-start.46
  39.8 7.4 copy-start.48
  39.8 7.4 copy-start.50
  39.9 7.4 copy-start.52
  39.9 7.4 copy-start.54
  39.9 7.4 copy-start.56
  40.8 6.5 copy-start.14
  40.8 6.5 copy-start.16
  40.8 6.5 copy-start.18
  40.8 6.5 copy-start.20
  40.8 6.5 copy-start.22
  40.8 6.5 copy-start.24
  40.8 6.5 copy-start.26
  40.9 6.5 copy-start.58
  40.9 6.5 copy-start.60
  40.9 6.5 copy-start.62
  40.9 6.5 copy-start.64
  40.9 6.5 copy-start.66
  40.9 6.5 copy-start.68
  40.9 6.5 copy-start.70
  270.3 249.7 %copy-start.84 = (f32[256]{0:T(256)}, f32[256]{0:T(256)S(1)}, u32[]{:S(2)}) copy-start(f32[256]{0:T(256)S(1)} %get-tuple-element.67) | copy-start | bytes 3076
  270.3 253.2 %copy-start.83 = (f32[256]{0:T(256)}, f32[256]{0:T(256)S(1)}, u32[]{:S(2)}) copy-start(f32[256]{0:T(256)S(1)} %get-tuple-element.66) | copy-start | bytes 3076
  524.0 2.3 copy-start.15
  524.0 2.3 copy-start.17
  524.0 2.3 copy-start.19
  524.0 2.3 copy-start.21
  524.0 2.3 copy-start.23
  524.0 2.3 copy-start.25
  524.0 2.3 copy-start.27
  524.1 2.3 copy-start.29
  524.1 2.3 copy-start.31
  524.1 2.3 copy-start.34
  524.1 2.3 copy-start.37
  524.1 2.3 copy-start.39
  524.1 2.3 copy-start.41
  524.1 2.3 copy-start.43
  524.1 2.3 copy-start.45
  524.1 2.3 copy-start.47
  524.1 2.3 copy-start.49
  524.2 2.3 copy-start.51
  536.7 2.5 copy-start.2
  536.7 2.5 copy-start.35
  536.7 5.0 copy-start.3
  536.7 5.0 copy-start.32
  536.8 314.7 %all-gather.4.cloned.1.call-start = ((), (), s32[]{:S(2)}) async-start(), calls=%async_computation.3 | async-start | bytes 4227072 | tf_op jit(solution)/shard_map/all_gather | solution.py:77
  536.8 5.0 copy-start.4
  536.8 5.0 copy-start.5
  536.8 4.9 copy-start.6
  536.8 4.9 copy-start.7
  536.9 4.9 copy-start.8
  536.9 4.9 copy-start.9
  536.9 4.9 copy-start.10
  548.2 330.9 %reduce-scatter.5.cloned.1.call-start = ((), (), s32[]{:S(2)}) async-start(), calls=%async_computation.2 | async-start | bytes 655360 | tf_op jit(solution)/shard_map/reduce_scatter | solution.py:92
  (25 other events, 51.9 us)
Sparse Core Ops, SparseCore 0:
  536.9 229.2 reduce-scatter.6
  769.9 81.5 all-gather.3
  854.9 24.2 reduce-scatter.4
